TPU v7x, 256 devices: a whole 4x4x8 slice. The times are simulated.
256 devices in a mesh: tm: 8 (over z), row: 8 (over x, core), obs: 4 (over y).
Axes of the slice: x: 4, y: 4, z: 8, core: 2. Of those that a mesh axis runs over, the one named last changes fastest.
Arguments:
- dyn_pattern: int32 [16, 8, 3], P('tm'), may hold values from 0 to 7
- dyn_values: float32 [16, 1024, 384], P('tm', ('row', 'obs')), may hold values from -0.3125 to 0.3125
- offsets: float32 [16, 1024], P('tm', ('row', 'obs')), may hold values from -6 to 6
- covariance: float32 [16, 1024, 1024], P('tm', ('row', 'obs')), may hold values from -1 to 14, as said below
- obs_block: int32 [16, 128], P('tm'), may hold values from 0 to 7
- obs_matrix: float32 [16, 128, 256], P('tm', 'obs'), may hold values from -0.375 to 0.375
- obs_data: float32 [16, 128], P('tm', 'obs'), may hold values from -6 to 6
Outputs:
- scan_dynamics: float32 [8, 1024, 1024], P('tm', ('row', 'obs'))
- scan_offset: float32 [8, 1024], P('tm', ('row', 'obs'))
- scan_covariance: float32 [8, 1024, 1024], P('tm', ('row', 'obs'))
- scan_factor: float32 [8, 1024, 512], P('tm', ('row', 'obs'))
- scan_information: float32 [8, 1024], P('tm', ('row', 'obs'))
Inputs may be any that keep to these rules, and one draw needn't show every extreme that they name: `dyn_pattern`: each entry names a block column. `obs_block`: each entry names a state block. Each covariance is symmetric and positive definite.
All inputs are finite; a program needn't handle non-finite values.
Results may differ from a plain program's by a relative error of at most 0.00019.
Values sent between devices are 32-bit elements; how exact they have to be, the bound alone decides.
A program may use at most 128 MiB of HBM per device.

v0:
```python
import jax
import jax.numpy as jnp
from jax import lax
from jax.sharding import PartitionSpec as P

largest_value = lax.Precision.HIGHEST


def shifted(block, axis, distance):
    devices = range(lax.axis_size(axis))
    route = [(i - distance, i) for i in devices if i - distance in devices]
    return lax.ppermute(block, axis, route)


def product(left, right):
    return jnp.dot(left, right, precision=largest_value, preferred_element_type=jnp.float32)


def lower_solve(lower, rhs):
    return lax.linalg.triangular_solve(lower, rhs, left_side=True, lower=True)


def assemble_dynamics(pattern, values):
    number_of_blocks = pattern.shape[0]
    per_row = pattern.shape[1]
    states = values.shape[0]
    block_extent = states // number_of_blocks
    indicator_matrix = (
        pattern[:, :, None] == jnp.arange(number_of_blocks, dtype=jnp.int32)[None, None, :]
    ).astype(jnp.float32)
    blocks = values.reshape(number_of_blocks, block_extent, per_row, block_extent)
    return jnp.einsum("ckd,cikj->cidj", indicator_matrix, blocks, precision=largest_value).reshape(
        states, states
    )


def assemble_factor(indices, matrix, number_of_blocks):
    item_count = matrix.shape[0]
    block_extent = matrix.shape[1] // 2
    reach = (indices[:, None] + jnp.arange(2, dtype=jnp.int32)[None, :]) % number_of_blocks
    indicator_matrix = (
        reach[:, :, None] == jnp.arange(number_of_blocks, dtype=jnp.int32)[None, None, :]
    ).astype(jnp.float32)
    piece_list = matrix.reshape(item_count, 2, block_extent)
    return jnp.einsum(
        "onr,onz->rzo", indicator_matrix, piece_list, precision=largest_value
    ).reshape(number_of_blocks * block_extent, item_count)


def combine(
    prior_dyn,
    prior_offsets,
    prior_cov,
    prior_factor,
    prior_zeta,
    own_dyn,
    own_offsets,
    own_cov,
    own_factor,
    own_zeta,
    row_start,
):
    panel_rows = prior_cov.shape[0]
    rank_width = own_factor.shape[1]
    own_pan = lax.dynamic_slice_in_dim(own_dyn, row_start, panel_rows, 0)
    gain_pan = product(prior_cov, own_factor)
    gain_rows = lax.all_gather(gain_pan, ("row", "obs"), axis=0, tiled=True)
    identity = jnp.eye(rank_width, dtype=jnp.float32)
    factor_pan = lax.dynamic_slice_in_dim(own_factor, row_start, panel_rows, 0)
    system = identity + lax.psum(product(factor_pan.T, gain_pan), ("row", "obs"))
    lower = jnp.linalg.cholesky(system)
    carried = product(own_dyn, gain_rows)
    observed = product(prior_dyn.T, own_factor)
    upper_part = lower_solve(lower, observed.T)
    weights = lower_solve(lower, carried.T).T
    weight_pan = lax.dynamic_slice_in_dim(weights, row_start, panel_rows, 0)
    spread_pan = product(prior_cov, own_dyn.T)
    moved = product(own_pan, lax.all_gather(spread_pan, ("row", "obs"), axis=0, tiled=True))
    new_dyn = product(own_pan, prior_dyn) - product(weight_pan, upper_part)
    new_cov = moved - product(weight_pan, weights.T) + own_cov
    residual = own_zeta - product(own_factor.T, prior_offsets)
    solved = lower_solve(lower, residual[:, None])[:, 0]
    new_offsets = product(own_pan, prior_offsets) + product(weight_pan, solved) + own_offsets
    upper_pan = lax.dynamic_slice_in_dim(upper_part, row_start, panel_rows, 1).T
    new_factor = jnp.concatenate([upper_pan, prior_factor], axis=1)
    new_zeta = jnp.concatenate([solved, prior_zeta])
    return (new_dyn, new_offsets, new_cov, new_factor, new_zeta)


def per_device(dyn_pattern, dyn_values, offsets, covariance, obs_block, obs_matrix, obs_data):
    panel_rows = covariance.shape[1]
    row_start = lax.axis_index(("row", "obs")) * panel_rows
    number_of_blocks = dyn_pattern.shape[1]
    obs_rows, obs_values = (
        lax.all_gather(obs_matrix, "obs", axis=1, tiled=True),
        lax.all_gather(obs_data, "obs", axis=1, tiled=True),
    )
    row_values, row_offsets = (
        lax.all_gather(dyn_values, ("row", "obs"), axis=1, tiled=True),
        lax.all_gather(offsets, ("row", "obs"), axis=1, tiled=True),
    )
    first_dyn = assemble_dynamics(dyn_pattern[0], row_values[0])
    second_dyn = assemble_dynamics(dyn_pattern[1], row_values[1])
    first_factor = assemble_factor(obs_block[0], obs_rows[0], number_of_blocks)
    second_factor = assemble_factor(obs_block[1], obs_rows[1], number_of_blocks)
    first_pan = lax.dynamic_slice_in_dim(first_factor, row_start, panel_rows, 0)
    dyn_pan, off_pan, cov_pan, fac_pan, zeta_full = combine(
        first_dyn,
        row_offsets[0],
        covariance[0],
        first_pan,
        obs_values[0],
        second_dyn,
        offsets[1],
        covariance[1],
        second_factor,
        obs_values[1],
        row_start,
    )
    later_pan, later_cov, later_off, later_fac, later_zeta = shifted(
        (dyn_pan, cov_pan, off_pan, fac_pan, zeta_full), "tm", -1
    )
    prior_full, later_full, later_factor, prior_offsets = (
        lax.all_gather(dyn_pan, ("row", "obs"), axis=0, tiled=True),
        lax.all_gather(later_pan, ("row", "obs"), axis=0, tiled=True),
        lax.all_gather(later_fac, ("row", "obs"), axis=0, tiled=True),
        lax.all_gather(off_pan, ("row", "obs"), axis=0, tiled=True),
    )
    top_dyn, top_off, top_cov, top_fac, top_zeta = combine(
        prior_full,
        prior_offsets,
        cov_pan,
        fac_pan,
        zeta_full,
        later_full,
        later_off,
        later_cov,
        later_factor,
        later_zeta,
        row_start,
    )
    even_turn = lax.axis_index("tm") % 2 == 0
    padded_fac = jnp.concatenate([fac_pan, jnp.zeros_like(fac_pan)], axis=1)
    padded_zeta = jnp.concatenate([zeta_full, jnp.zeros_like(zeta_full)])
    out_dyn = jnp.where(even_turn, top_dyn, dyn_pan)
    out_off = jnp.where(even_turn, top_off, off_pan)
    out_cov = jnp.where(even_turn, top_cov, cov_pan)
    out_fac = jnp.where(even_turn, top_fac, padded_fac)
    out_zeta = jnp.where(even_turn, top_zeta, padded_zeta)
    output_information = product(out_fac, out_zeta)
    return (out_dyn[None], out_off[None], out_cov[None], out_fac[None], output_information[None])


def solution(mesh):
    placed = (
        P("tm", None, None),
        P("tm", ("row", "obs"), None),
        P("tm", ("row", "obs")),
        P("tm", ("row", "obs"), None),
        P("tm", None),
        P("tm", "obs", None),
        P("tm", "obs"),
    )
    return jax.shard_map(
        per_device,
        mesh=mesh,
        in_specs=placed,
        out_specs=(
            P("tm", ("row", "obs"), None),
            P("tm", ("row", "obs")),
            P("tm", ("row", "obs"), None),
            P("tm", ("row", "obs"), None),
            P("tm", ("row", "obs")),
        ),
        check_vma=False,
    )
```

profile of v0, /device:TPU:1, one launch (start us, length us, event | category | flops | bytes accessed | tf_op | source)
XLA Modules:
  0.0 616.6 jit_solution(8064863237237655006)
XLA Ops:
  7.2 0.7 all-gather.10.cloned.1.call-update
  8.0 11.5 %all_gather.37 = f32[2,128,256]{2,1,0:T(8,128)S(1)} all-gather(f32[2,32,256]{2,1,0:T(8,128)} %param.16), channel_id=1, replica_groups=mesh['tm'=8,'row'=8,'obs'=4] {'obs'}, dimensions={1}, use_global_device_ids=true | all-gather | bytes 327680 | tf_op jit(solution)/shard_map/all_gather | solution.py:95
  19.5 0.8 slice_bitcast_fusion.12
  20.4 0.9 fusion.36
  21.4 1.5 fusion.42
  23.0 0.9 fusion.83
  24.0 40.9 %all-gather.10.cloned.1.call-done = f32[2,1024,384]{2,1,0:T(8,128)} async-done(((f32[2,32,384]{2,1,0:T(8,128)}), f32[2,1024,384]{2,1,0:T(8,128)}) %all-gather.10.cloned.1.call-update) | async-done | bytes 3145744 | tf_op jit(solution)/shard_map/all_gather | solution.py:99
  64.9 3.2 fusion.135
  68.2 3.6 reshape.312
  71.8 4.3 fusion.104
  76.1 2.0 copy-done
  78.1 4.9 convolution_bitcast_fusion.1
  83.5 0.9 convolution_bitcast_fusion
  84.7 89.2 %all-reduce.5.cloned.1.call-done = f32[128,128]{1,0:T(8,128)} async-done(((f32[128,128]{1,0:T(8,128)}), f32[128,128]{1,0:T(8,128)}) %all-reduce.5.cloned.1.call-update) | async-done | bytes 65552 | tf_op jit(solution)/shard_map/psum | solution.py:70
  173.8 0.9 convert_add_fusion.1
  174.8 0.9 fusion.77
  175.6 11.7 %cholesky.60 = f32[128,128]{1,0:T(8,128)S(1)} custom-call(f32[128,128]{1,0:T(8,128)S(1)} %fusion.77), custom_call_target="Cholesky" | custom-call | tf_op jit(solution)/shard_map/jit(cholesky)/cholesky | solution.py:71
  188.0 0.7 fusion.55
  188.7 9.8 %custom-call.31 = f32[1,128,128]{1,2,0:T(8,128)S(1)} custom-call(f32[1,128,128]{2,1,0:T(8,128)S(1)} %fusion.55), custom_call_target="InvertDiagBlocksLowerTriangular" | custom-call | tf_op jit(solution)/shard_map/triangular_solve/custom-call.4 | solution.py:20
  198.5 2.2 reshape.313
  200.7 4.3 fusion.107
  205.1 2.0 copy-done.2
  207.1 3.0 fusion
  210.9 1.3 collective-permute-start.1
  212.1 3.8 collective-permute-done.1
  216.6 42.6 %all_gather.38 = f32[1024,128]{1,0:T(8,128)S(1)} all-gather(f32[32,128]{1,0:T(8,128)S(1)} %bitcast.273), channel_id=1, replica_groups=mesh['tm'=8,'row'=8,'obs'=4] {'row','obs'}, dimensions={0}, use_global_device_ids=true | all-gather | bytes 540672 | tf_op jit(solution)/shard_map/all_gather | solution.py:67
  259.2 3.4 copy.79
  262.6 4.8 fusion.133
  268.5 3.0 fusion.6
  271.5 1.4 collective-permute-start
  273.0 4.4 collective-permute-done
  277.4 0.7 copy-done.12
  278.9 4.8 fusion.52
  284.2 1.9 fusion.138
  286.1 1.9 fusion.100
  288.1 0.7 all-gather.20.cloned.1.call-update
  288.9 40.2 %all-gather = f32[32,32,2]{1,2,0:T(2,128)S(1)} all-gather(f32[1,32,2]{1,2,0:T(2,128)S(1)} %bitcast.282), channel_id=1, replica_groups=mesh['tm'=8,'row'=8,'obs'=4] {'row','obs'}, dimensions={0}, use_global_device_ids=true | all-gather | bytes 8448 | tf_op jit(solution)/shard_map/all_gather | solution.py:100
  329.1 5.2 all-gather.1
  334.5 0.7 fusion.175
  335.7 6.7 %fusion.141 = f32[32,1024]{1,0:T(8,128)} fusion(f32[32,1024]{1,0:T(8,128)S(1)} %fusion.12, f32[1024,1024]{1,0:T(8,128)} %all-gather.12.cloned.1.call-done), kind=kOutput, calls=%fused_computation.205 | convolution fusion | flops 402653184 | bytes 4456448 | tf_op jit(solution)/shard_map/dot_general | solution.py:16
  343.9 1.3 collective-permute-start.2
  345.3 1.1 convolution_bitcast_fusion.9
  346.6 1.3 collective-permute-start.3
  348.2 63.2 %all-reduce.1 = f32[1024]{0:T(1024)S(1)} all-reduce(f32[1024]{0:T(1024)S(1)} %dynamic-update-slice.17), channel_id=1, replica_groups=mesh['tm'=8,'row'=8,'obs'=4] {'row','obs'}, use_global_device_ids=true, to_apply=%add.1 | all-reduce | flops 1024 | bytes 8192
  412.1 1.3 collective-permute-start.4
  413.4 6.0 fusion.140
  419.4 80.5 %all-reduce.7.cloned.1.call-done = f32[256,256]{0,1:T(8,128)} async-done(((f32[256,256]{0,1:T(8,128)}), f32[256,256]{0,1:T(8,128)}) %all-reduce.7.cloned.1.call-update) | async-done | bytes 262160 | tf_op jit(solution)/shard_map/psum | solution.py:70
  499.9 1.0 convert_add_fusion
  501.0 1.0 fusion.34
  502.0 11.7 %cholesky.115 = f32[128,128]{1,0:T(8,128)S(1)} custom-call(f32[128,128]{1,0:T(8,128)S(1)} %cholesky.141), custom_call_target="Cholesky" | custom-call | tf_op jit(solution)/shard_map/jit(cholesky)/cholesky | solution.py:71
  513.8 9.8 %custom-call.26 = f32[1,128,128]{1,2,0:T(8,128)S(1)} custom-call(f32[1,128,128]{2,1,0:T(8,128)S(1)} %get-tuple-element.62), custom_call_target="InvertDiagBlocksLowerTriangular" | custom-call | tf_op jit(solution)/shard_map/jit(cholesky)/cholesky | solution.py:71
  524.1 11.7 %cholesky.128 = f32[128,128]{1,0:T(8,128)S(1)} custom-call(f32[128,128]{1,0:T(8,128)S(1)} %convolution_subtract_fusion.3), custom_call_target="Cholesky" | custom-call | tf_op jit(solution)/shard_map/jit(cholesky)/cholesky | solution.py:71
  538.5 4.0 while.5
  539.1 1.4 bitcast_dynamic-update-slice_fusion.2
  541.1 1.4 bitcast_dynamic-update-slice_fusion.2
  542.5 19.8 %custom-call.33 = f32[2,128,128]{1,2,0:T(8,128)S(1)} custom-call(f32[2,128,128]{2,1,0:T(8,128)S(1)} %get-tuple-element.29), custom_call_target="InvertDiagBlocksLowerTriangular" | custom-call | tf_op jit(solution)/shard_map/triangular_solve/custom-call.5 | solution.py:20
  565.1 0.7 fusion.60
  566.5 9.2 %fusion.139 = f32[256,1024]{1,0:T(8,128)S(1)} fusion(f32[1024,256]{1,0:T(8,128)} %all-gather.20.cloned.1.call-done, f32[1024,1024]{1,0:T(8,128)} %all-gather.12.cloned.1.call-done), kind=kOutput, calls=%fused_computation.203 | convolution fusion | flops 3221225472 | bytes 6291456 | tf_op jit(solution)/shard_map/dot_general | solution.py:16
  577.7 0.7 fusion.24
  578.4 0.7 fusion.23
  579.2 4.1 fusion.14
  583.4 1.7 fusion.20
  585.1 19.4 %all-gather.22.cloned.1.call-done = f32[1024,1024]{1,0:T(8,128)} async-done(((f32[32,1024]{1,0:T(8,128)}), f32[1024,1024]{1,0:T(8,128)}) %all-gather.22.cloned.1.call-update) | async-done | bytes 4194320 | tf_op jit(solution)/shard_map/all_gather | solution.py:78
  604.5 5.4 fusion.11
  (127 shorter events, 17.6 us)
Async XLA Ops:
  7.2 16.8 %copy-start.15 = (s32[2,8,3]{1,0,2:T(2,128)S(1)}, s32[2,8,3]{1,0,2:T(2,128)}, u32[]{:S(2)}) copy-start(s32[2,8,3]{1,0,2:T(2,128)} %param.11) | copy-start | bytes 580
  7.2 57.8 %all-gather.10.cloned.1.call-start = ((), (), s32[]{:S(2)}) async-start(), calls=%async_computation | async-start | bytes 3244032 | tf_op jit(solution)/shard_map/all_gather | solution.py:99
  7.9 165.9 %all-reduce.5.cloned.1.call-start = ((), (), s32[]{:S(2)}) async-start(), calls=%async_computation.1 | async-start | bytes 131072 | tf_op jit(solution)/shard_map/psum | solution.py:70
  23.9 255.0 %all-gather.18.cloned.1.call-start = ((), (), s32[]{:S(2)}) async-start(), calls=%async_computation.5 | async-start | bytes 4325376 | tf_op jit(solution)/shard_map/all_gather | solution.py:78
  68.2 9.9 %copy-start.10 = (f32[2,32,1024]{2,1,0:T(8,128)S(1)}, f32[2,32,1024]{2,1,0:T(8,128)}, u32[]{:S(2)}) copy-start(f32[2,32,1024]{2,1,0:T(8,128)} %param.14) | copy-start | bytes 786436
  76.1 2.0 copy-start
  83.0 201.2 %all-gather.16.cloned.1.call-start = ((), (), s32[]{:S(2)}) async-start(), calls=%async_computation.4 | async-start | bytes 1081344 | tf_op jit(solution)/shard_map/all_gather | solution.py:126
  84.6 120.4 %copy-start.9 = (f32[8,128,128]{2,1,0:T(8,128)}, f32[8,128,128]{2,1,0:T(8,128)S(1)}, u32[]{:S(2)}) copy-start(f32[8,128,128]{2,1,0:T(8,128)S(1)} %copy.56) | copy-start | bytes 1572868
  205.0 2.0 copy-start.2
  210.9 5.0 collective-permute-start.1
  215.9 0.6 copy-start.13
  216.5 119.2 %all-gather.12.cloned.1.call-start = ((), (), s32[]{:S(2)}) async-start(), calls=%async_computation.2 | async-start | bytes 4325376 | tf_op jit(solution)/shard_map/all_gather | solution.py:125
  259.2 3.5 copy-start.1
  262.6 5.9 copy-start.6
  262.6 5.9 copy-start.3
  271.5 6.6 %copy-start.7 = (f32[32,1024]{1,0:T(8,128)}, f32[32,1024]{1,0:T(8,128)S(1)}, u32[]{:S(2)}) copy-start(f32[32,1024]{1,0:T(8,128)S(1)} %fusion.6) | copy-start | bytes 393220
  271.5 17.3 %copy-start.14 = (f32[2,32]{1,0:T(2,128)S(1)}, f32[2,32]{1,0:T(2,128)}, u32[]{:S(2)}) copy-start(f32[2,32]{1,0:T(2,128)} %param.13) | copy-start | bytes 772
  271.5 57.6 %copy-start.16 = (f32[2,32]{1,0:T(2,128)S(1)}, f32[2,32]{1,0:T(2,128)}, u32[]{:S(2)}) copy-start(f32[2,32]{1,0:T(2,128)} %param.17) | copy-start | bytes 772
  271.5 5.8 collective-permute-start
  277.4 0.7 copy-start.12
  278.1 135.3 %all-gather.14.cloned.1.call-start = ((), (), s32[]{:S(2)}) async-start(), calls=%async_computation.3 | async-start | bytes 4325376 | tf_op jit(solution)/shard_map/all_gather | solution.py:124
  278.6 221.2 %all-reduce.7.cloned.1.call-start = ((), (), s32[]{:S(2)}) async-start(), calls=%async_computation.6 | async-start | bytes 524288 | tf_op jit(solution)/shard_map/psum | solution.py:70
  283.7 58.8 %copy-start.17 = (u32[256]{0:T(256)S(1)}, u32[256]{0:T(256)}, u32[]{:S(2)}) copy-start(u32[256]{0:T(256)} %constant.217) | copy-start | bytes 3076
  284.2 127.2 %copy-start.5 = (f32[1024,256]{1,0:T(8,128)S(1)}, f32[1024,256]{1,0:T(8,128)}, u32[]{:S(2)}) copy-start(f32[1024,256]{1,0:T(8,128)} %all-gather.16.cloned.1.call-done) | copy-start | bytes 3145732
  286.1 2.0 copy-start.11
  288.1 278.4 %all-gather.20.cloned.1.call-start = ((), (), s32[]{:S(2)}) async-start(), calls=%async_computation.7 | async-start | bytes 1081344 | tf_op jit(solution)/shard_map/all_gather | solution.py:67
  288.8 315.7 %all-gather.22.cloned.1.call-start = ((), (), s32[]{:S(2)}) async-start(), calls=%async_computation.8 | async-start | bytes 4325376 | tf_op jit(solution)/shard_map/all_gather | solution.py:78
  343.9 68.2 %collective-permute-start.2 = (f32[256]{0:T(256)S(1)}, f32[256]{0:T(256)S(1)}, u32[]{:S(2)}, u32[]{:S(2)}) collective-permute-start(f32[256]{0:T(256)S(1)} %pad_maximum_fusion.5), channel_id=1, source_target_pairs={{32,0},{64,32},{96,64},{128,96},{160,128},{192,160},{224,192},{33,... | collective-permute-start | bytes 3080 | tf_op jit(solution)/shard_map/ppermute | solution.py:12
  346.6 236.8 %collective-permute-start.3 = (f32[32]{0:T(128)S(1)}, f32[32]{0:T(128)S(1)}, u32[]{:S(2)}, u32[]{:S(2)}) collective-permute-start(f32[32]{0:T(128)S(1)} %fusion.16), channel_id=1, source_target_pairs={{32,0},{64,32},{96,64},{128,96},{160,128},{192,160},{224,192},{33,... | collective-permute-start | bytes 392 | tf_op jit(solution)/shard_map/ppermute | solution.py:12
  412.1 173.0 %collective-permute-start.4 = (f32[32,1024]{1,0:T(8,128)S(1)}, f32[32,1024]{1,0:T(8,128)S(1)}, u32[]{:S(2)}, u32[]{:S(2)}) collective-permute-start(f32[32,1024]{1,0:T(8,128)S(1)} %fusion.12), channel_id=1, source_target_pairs={{32,0},{64,32},{96,64},{128,96},{160,128},{192,160},{224,192},{33,... | collective-permute-start | bytes 393224 | tf_op jit(solution)/shard_map/ppermute | solution.py:12
  575.7 3.5 copy-start.4
  575.7 3.5 copy-start.8
Sparse Core Ops, SparseCore 0:
  10.6 54.3 all-gather.9
  68.8 104.9 all-reduce.4
  177.3 50.7 all-gather.17
  231.4 47.2 all-gather.15
  281.4 50.4 all-gather.11
  335.2 50.5 all-gather.13
  389.4 110.4 all-reduce.6
  503.0 48.6 all-gather.19
  554.3 50.1 all-gather.21
where the time goes:
time: 624 us; the launch traced here: 617 us
  waiting for transfers between devices  240 us (38%)
  blocking collectives  163 us (26%)
  other arithmetic  82 us (13%)
  matrix products  81.8 us (13%)
  local copies, waits for them, and re-layouts  25.7 us (4%)
  between operations  16.7 us (3%)
  starting transfers between devices  7.45 us (1%)
    psum x2, waiting for transfers between devices, combine(): lax.psum(product(factor_pan.T, gain_pan), ('row', 'obs'))  170 us
    dot_general x25, matrix products, product(): jnp.dot(left, right, precision=largest_value, preferred_element_type=jnp....  65.3 us
    unnamed x1, blocking collectives  63.2 us
    another operation x10, other arithmetic, combine(): lower = jnp.linalg.cholesky(system)  47 us
    all_gather x1, blocking collectives, combine(): gain_rows = lax.all_gather(gain_pan, ('row', 'obs'), axis=0, tiled=True)  42.6 us
    all_gather x1, waiting for transfers between devices, per_device(): lax.all_gather(dyn_values, ('row', 'obs'), axis=1, tiled=True)  40.9 us
    all_gather x1, blocking collectives, per_device(): lax.all_gather(offsets, ('row', 'obs'), axis=1, tiled=True)  40.2 us
    another operation x8, other arithmetic, lower_solve(): return lax.linalg.triangular_solve(lower, rhs, left_side=True, lower=True)  30.5 us
  transfers between devices with their start and end apart: 14, of which 6 were waited for; matrix products, arithmetic and copies ran while one was open for 29% of the time, Pallas kernels for 0%

commit v1 on v0

--- a/solution.py
+++ b/solution.py
@@ -2,6 +2,7 @@
 import jax.numpy as jnp
 from jax import lax
 from jax.sharding import PartitionSpec as P
+from jax.lax import all_gather
 
 largest_value = lax.Precision.HIGHEST
 
@@ -67,7 +68,10 @@
     gain_rows = lax.all_gather(gain_pan, ("row", "obs"), axis=0, tiled=True)
     identity = jnp.eye(rank_width, dtype=jnp.float32)
     factor_pan = lax.dynamic_slice_in_dim(own_factor, row_start, panel_rows, 0)
-    system = identity + lax.psum(product(factor_pan.T, gain_pan), ("row", "obs"))
+    begin_the_cycles = lambda incoming_x, along_axis: jnp.sum(
+        all_gather(incoming_x, along_axis), axis=0
+    )
+    system = identity + begin_the_cycles(product(factor_pan.T, gain_pan), ("row", "obs"))
     lower = jnp.linalg.cholesky(system)
     carried = product(own_dyn, gain_rows)
     observed = product(prior_dyn.T, own_factor)

time: 624 us -> 542 us (0.87)
  waiting for transfers between devices: 240 us -> 146 us
    psum x2 -> x0, waiting for transfers between devices: 170 us -> none  [combine(): lax.psum(product(factor_pan.T, gain_pan), ('row', 'obs'))]
    all_gather x0 -> x2, waiting for transfers between devices: none -> 82.1 us  [combine(): all_gather(incoming_x, along_axis)]
    all_gather x2, waiting for transfers between devices: 19.4 us -> 0.02 us  [combine(): lax.all_gather(spread_pan, ('row', 'obs'), axis=0, tiled=True)]
    all_gather x1, waiting for transfers between devices: 0.01 us -> 13.2 us  [combine(): gain_rows = lax.all_gather(gain_pan, ('row', 'obs'), axis=0, tiled=True)]
  transfers between devices with their start and end apart: 14 -> 14, of which waited for: 6 -> 6; matrix products, arithmetic and copies ran while one was open for 29% -> 36% of each run, Pallas kernels for 0% -> 0%
where the time goes in v1:
time: 542 us; the launch traced here: 535 us
  blocking collectives  162 us (30%)
  waiting for transfers between devices  146 us (27%)
  matrix products  87.2 us (16%)
  other arithmetic  86.7 us (16%)
  local copies, waits for them, and re-layouts  28.8 us (5%)
  between operations  16.8 us (3%)
  starting transfers between devices  7.44 us (1%)
    all_gather x2, waiting for transfers between devices, combine(): all_gather(incoming_x, along_axis)  82.1 us
    dot_general x25, matrix products, product(): jnp.dot(left, right, precision=largest_value, preferred_element_type=jnp....  66.3 us
    unnamed x1, blocking collectives  61.9 us
    another operation x10, other arithmetic, combine(): lower = jnp.linalg.cholesky(system)  47 us
    all_gather x1, blocking collectives, combine(): gain_rows = lax.all_gather(gain_pan, ('row', 'obs'), axis=0, tiled=True)  42.3 us
    all_gather x1, waiting for transfers between devices, per_device(): lax.all_gather(dyn_values, ('row', 'obs'), axis=1, tiled=True)  40.9 us
    all_gather x1, blocking collectives, per_device(): lax.all_gather(offsets, ('row', 'obs'), axis=1, tiled=True)  40.3 us
    another operation x8, other arithmetic, lower_solve(): return lax.linalg.triangular_solve(lower, rhs, left_side=True, lower=True)  31.8 us
  transfers between devices with their start and end apart: 14, of which 6 were waited for; matrix products, arithmetic and copies ran while one was open for 36% of the time, Pallas kernels for 0%

profile of v1, /device:TPU:1, one launch (start us, length us, event | category | flops | bytes accessed | tf_op | source)
XLA Modules:
  0.0 534.5 jit_solution(10680094058715168137)
XLA Ops:
  8.0 11.5 %all_gather.49 = f32[2,128,256]{2,1,0:T(8,128)S(1)} all-gather(f32[2,32,256]{2,1,0:T(8,128)} %param.16), channel_id=1, replica_groups=mesh['tm'=8,'row'=8,'obs'=4] {'obs'}, dimensions={1}, use_global_device_ids=true | all-gather | bytes 327680 | tf_op jit(solution)/shard_map/all_gather | solution.py:99
  19.5 0.8 slice_bitcast_fusion.12
  20.4 0.9 fusion.37
  21.4 1.5 fusion.43
  23.0 0.9 fusion.85
  24.0 40.9 %all-gather.14.cloned.1.call-done = f32[2,1024,384]{2,1,0:T(8,128)} async-done(((f32[2,32,384]{2,1,0:T(8,128)}), f32[2,1024,384]{2,1,0:T(8,128)}) %all-gather.14.cloned.1.call-update) | async-done | bytes 3145744 | tf_op jit(solution)/shard_map/all_gather | solution.py:103
  64.9 3.2 fusion.137
  68.2 3.6 reshape.314
  71.8 4.3 fusion.106
  76.1 2.0 copy-done
  78.1 4.9 convolution_bitcast_fusion.1
  83.5 0.9 convolution_bitcast_fusion
  84.7 31.7 %all-gather.28.cloned.1.call-done = f32[4096,128]{1,0:T(8,128)} async-done(((f32[128,128]{1,0:T(8,128)}), f32[4096,128]{1,0:T(8,128)}) %all-gather.28.cloned.1.call-update) | async-done | bytes 2097168 | tf_op jit(solution)/shard_map/all_gather | solution.py:72
  116.4 1.7 reduce_sum.22
  118.2 11.7 %cholesky.60 = f32[128,128]{1,0:T(8,128)S(1)} custom-call(f32[128,128]{1,0:T(8,128)S(1)} %fusion.79), custom_call_target="Cholesky" | custom-call | tf_op jit(solution)/shard_map/jit(cholesky)/cholesky | solution.py:75
  131.3 9.8 %custom-call.31 = f32[1,128,128]{1,2,0:T(8,128)S(1)} custom-call(f32[1,128,128]{2,1,0:T(8,128)S(1)} %fusion.56), custom_call_target="InvertDiagBlocksLowerTriangular" | custom-call | tf_op jit(solution)/shard_map/triangular_solve/custom-call.4 | solution.py:21
  141.1 2.2 reshape.315
  143.3 4.3 fusion.109
  147.6 2.0 copy-done.2
  149.7 3.0 fusion
  153.4 1.3 collective-permute-start.1
  154.7 3.8 collective-permute-done.1
  159.2 42.3 %all_gather.52 = f32[1024,128]{1,0:T(8,128)S(1)} all-gather(f32[32,128]{1,0:T(8,128)S(1)} %bitcast.281), channel_id=1, replica_groups=mesh['tm'=8,'row'=8,'obs'=4] {'row','obs'}, dimensions={0}, use_global_device_ids=true | all-gather | bytes 540672 | tf_op jit(solution)/shard_map/all_gather | solution.py:68
  201.5 3.4 copy.75
  204.9 4.8 fusion.135
  210.9 3.0 fusion.6
  213.8 1.4 collective-permute-start
  215.3 4.4 collective-permute-done
  221.2 4.8 fusion.53
  226.5 2.5 fusion.140
  229.1 1.9 fusion.102
  231.1 40.3 %all-gather.2 = f32[32,32,2]{1,2,0:T(2,128)S(1)} all-gather(f32[1,32,2]{1,2,0:T(2,128)S(1)} %bitcast.290), channel_id=1, replica_groups=mesh['tm'=8,'row'=8,'obs'=4] {'row','obs'}, dimensions={0}, use_global_device_ids=true | all-gather | bytes 8448 | tf_op jit(solution)/shard_map/all_gather | solution.py:104
  271.5 5.9 %all-gather.3 = f32[4,32,2]{1,2,0:T(2,128)S(1)} all-gather(f32[1,32,2]{1,2,0:T(2,128)S(1)} %bitcast.296), channel_id=1, replica_groups=mesh['tm'=8,'row'=8,'obs'=4] {'obs'}, dimensions={0}, use_global_device_ids=true | all-gather | bytes 1280 | tf_op jit(solution)/shard_map/all_gather | solution.py:100
  277.5 1.3 fusion.177
  279.4 6.7 %fusion.143 = f32[32,1024]{1,0:T(8,128)} fusion(f32[32,1024]{1,0:T(8,128)S(1)} %fusion.12, f32[1024,1024]{1,0:T(8,128)} %all-gather.16.cloned.1.call-done), kind=kOutput, calls=%fused_computation.207 | convolution fusion | flops 402653184 | bytes 4456448 | tf_op jit(solution)/shard_map/dot_general | solution.py:17
  288.1 1.3 collective-permute-start.2
  290.1 1.1 convolution_bitcast_fusion.9
  291.2 0.9 fusion.16
  292.1 1.3 collective-permute-start.3
  293.4 0.9 dynamic-update-slice.17
  294.2 61.9 %all-reduce.1 = f32[1024]{0:T(1024)S(1)} all-reduce(f32[1024]{0:T(1024)S(1)} %dynamic-update-slice.17), channel_id=1, replica_groups=mesh['tm'=8,'row'=8,'obs'=4] {'row','obs'}, use_global_device_ids=true, to_apply=%add.1 | all-reduce | flops 1024 | bytes 8192
  357.3 1.3 collective-permute-start.4
  358.6 5.6 %fusion.142 = f32[256,1024]{1,0:T(8,128)S(1)} fusion(f32[1024,256]{1,0:T(8,128)S(1)} %copy-done.5, f32[1024,1024]{1,0:T(8,128)} %all-gather.18.cloned.1.call-done), kind=kOutput, calls=%fused_computation.206 | convolution fusion | flops 3221225472 | bytes 6291456 | tf_op jit(solution)/shard_map/dot_general | solution.py:17
  364.2 13.2 %all-gather.24.cloned.1.call-done = f32[1024,256]{1,0:T(8,128)} async-done(((f32[32,256]{1,0:T(8,128)}), f32[1024,256]{1,0:T(8,128)}) %all-gather.24.cloned.1.call-update) | async-done | bytes 1048592 | tf_op jit(solution)/shard_map/all_gather | solution.py:68
  377.4 9.4 %fusion.141 = f32[256,1024]{1,0:T(8,128)S(1)} fusion(f32[1024,256]{1,0:T(8,128)} %all-gather.24.cloned.1.call-done, f32[1024,1024]{1,0:T(8,128)} %all-gather.16.cloned.1.call-done), kind=kOutput, calls=%fused_computation.205 | convolution fusion | flops 3221225472 | bytes 6291456 | tf_op jit(solution)/shard_map/dot_general | solution.py:17
  386.9 50.4 %all-gather.30.cloned.1.call-done = f32[8192,256]{1,0:T(8,128)} async-done(((f32[256,256]{1,0:T(8,128)}), f32[8192,256]{1,0:T(8,128)}) %all-gather.30.cloned.1.call-update) | async-done | bytes 8388624 | tf_op jit(solution)/shard_map/all_gather | solution.py:72
  437.3 3.9 reduce_sum.24
  441.4 11.7 %cholesky.115 = f32[128,128]{1,0:T(8,128)S(1)} custom-call(f32[128,128]{1,0:T(8,128)S(1)} %cholesky.141), custom_call_target="Cholesky" | custom-call | tf_op jit(solution)/shard_map/jit(cholesky)/cholesky | solution.py:75
  453.2 9.8 %custom-call.26 = f32[1,128,128]{1,2,0:T(8,128)S(1)} custom-call(f32[1,128,128]{2,1,0:T(8,128)S(1)} %get-tuple-element.62), custom_call_target="InvertDiagBlocksLowerTriangular" | custom-call | tf_op jit(solution)/shard_map/jit(cholesky)/cholesky | solution.py:75
  463.5 11.7 %cholesky.128 = f32[128,128]{1,0:T(8,128)S(1)} custom-call(f32[128,128]{1,0:T(8,128)S(1)} %convolution_subtract_fusion.3), custom_call_target="Cholesky" | custom-call | tf_op jit(solution)/shard_map/jit(cholesky)/cholesky | solution.py:75
  477.9 5.2 while.5
  478.5 2.0 bitcast_dynamic-update-slice_fusion.2
  481.1 2.0 bitcast_dynamic-update-slice_fusion.2
  483.1 20.6 %custom-call.33 = f32[2,128,128]{1,2,0:T(8,128)S(1)} custom-call(f32[2,128,128]{2,1,0:T(8,128)} %get-tuple-element.29), custom_call_target="InvertDiagBlocksLowerTriangular" | custom-call | tf_op jit(solution)/shard_map/triangular_solve/custom-call.5 | solution.py:21
  505.0 1.5 fusion.27
  506.8 1.2 convolution_bitcast_fusion.5
  508.2 1.0 convolution_bitcast_fusion.3
  509.3 0.7 maximum_select_fusion.3
  510.0 1.5 fusion.31
  512.1 1.5 fusion.30
  515.8 0.7 fusion.23
  516.5 4.1 fusion.14
  520.8 1.7 fusion.20
  522.4 5.3 %fusion.11 = f32[1,32,1024]{2,1,0:T(8,128)} fusion(f32[32,1024]{1,0:T(8,128)S(1)} %fusion.12, f32[32,1024]{1,0:T(8,128)} %collective-permute-done.4, f32[32,1024]{1,0:T(8,128)S(1)} %fusion.24, f32[1024,1024]{1,0:T(8,128)} %all-gather.26.cloned.1.call-done, f32[1024,1024]{1,0:T(8,128)} %all-gather.16.cloned.1.call-done, s32[]{:T(128)S(6)} %select_n.93, ...), kind=kOutput, calls=%fused_computation.20 | convolution fusion | flops 402751488 | bytes 4849669 | tf_op jit(solution)/shard_map/dot_general | solution.py:17
  (147 shorter events, 20.0 us)
Async XLA Ops:
  7.2 16.8 %copy-start.23 = (s32[2,8,3]{1,0,2:T(2,128)S(1)}, s32[2,8,3]{1,0,2:T(2,128)}, u32[]{:S(2)}) copy-start(s32[2,8,3]{1,0,2:T(2,128)} %param.11) | copy-start | bytes 580
  7.2 57.8 %all-gather.14.cloned.1.call-start = ((), (), s32[]{:S(2)}) async-start(), calls=%async_computation | async-start | bytes 3244032 | tf_op jit(solution)/shard_map/all_gather | solution.py:103
  7.9 108.5 %all-gather.28.cloned.1.call-start = ((), (), s32[]{:S(2)}) async-start(), calls=%async_computation.7 | async-start | bytes 2162688 | tf_op jit(solution)/shard_map/all_gather | solution.py:72
  23.9 197.3 %all-gather.22.cloned.1.call-start = ((), (), s32[]{:S(2)}) async-start(), calls=%async_computation.4 | async-start | bytes 4325376 | tf_op jit(solution)/shard_map/all_gather | solution.py:82
  68.2 9.9 %copy-start.11 = (f32[2,32,1024]{2,1,0:T(8,128)S(1)}, f32[2,32,1024]{2,1,0:T(8,128)}, u32[]{:S(2)}) copy-start(f32[2,32,1024]{2,1,0:T(8,128)} %param.14) | copy-start | bytes 786436
  76.1 2.0 copy-start
  83.0 143.5 %all-gather.20.cloned.1.call-start = ((), (), s32[]{:S(2)}) async-start(), calls=%async_computation.3 | async-start | bytes 1081344 | tf_op jit(solution)/shard_map/all_gather | solution.py:130
  84.7 63.0 %copy-start.10 = (f32[8,128,128]{2,1,0:T(8,128)}, f32[8,128,128]{2,1,0:T(8,128)S(1)}, u32[]{:S(2)}) copy-start(f32[8,128,128]{2,1,0:T(8,128)S(1)} %copy.52) | copy-start | bytes 1572868
  84.7 68.7 %copy-start.14 = (f32[32,128]{1,0:T(8,128)}, f32[32,128]{1,0:T(8,128)S(1)}, u32[]{:S(2)}) copy-start(f32[32,128]{1,0:T(8,128)S(1)} %constant_dynamic-slice_fusion.1) | copy-start | bytes 49156
  147.6 2.0 copy-start.2
  153.4 5.1 collective-permute-start.1
  158.5 0.6 copy-start.20
  159.1 120.3 %all-gather.16.cloned.1.call-start = ((), (), s32[]{:S(2)}) async-start(), calls=%async_computation.1 | async-start | bytes 4325376 | tf_op jit(solution)/shard_map/all_gather | solution.py:129
  201.5 3.5 copy-start.1
  204.9 5.9 %copy-start.6 = (f32[128,8,8,128]{3,1,2,0:T(8,128)}, f32[128,8,8,128]{3,1,2,0:T(8,128)S(1)}, u32[]{:S(2)}) copy-start(f32[128,8,8,128]{3,1,2,0:T(8,128)S(1)} %copy.75) | copy-start | bytes 12582916
  204.9 5.9 %copy-start.3 = (f32[8,8,128,128]{3,1,2,0:T(8,128)S(1)}, f32[8,8,128,128]{3,1,2,0:T(8,128)}, u32[]{:S(2)}) copy-start(f32[8,8,128,128]{3,1,2,0:T(8,128)} %copy-done.2) | copy-start | bytes 12582916
  210.8 15.2 %copy-start.12 = (f32[2,32,1024]{2,1,0:T(8,128)S(1)}, f32[2,32,1024]{2,1,0:T(8,128)}, u32[]{:S(2)}) copy-start(f32[2,32,1024]{2,1,0:T(8,128)} %param.14) | copy-start | bytes 786436
  213.8 6.6 %copy-start.7 = (f32[32,1024]{1,0:T(8,128)}, f32[32,1024]{1,0:T(8,128)S(1)}, u32[]{:S(2)}) copy-start(f32[32,1024]{1,0:T(8,128)S(1)} %fusion.6) | copy-start | bytes 393220
  213.8 17.3 %copy-start.22 = (f32[2,32]{1,0:T(2,128)S(1)}, f32[2,32]{1,0:T(2,128)}, u32[]{:S(2)}) copy-start(f32[2,32]{1,0:T(2,128)} %param.13) | copy-start | bytes 772
  213.8 57.7 %copy-start.25 = (f32[2,32]{1,0:T(2,128)S(1)}, f32[2,32]{1,0:T(2,128)}, u32[]{:S(2)}) copy-start(f32[2,32]{1,0:T(2,128)} %param.17) | copy-start | bytes 772
  213.8 5.8 %collective-permute-start = (f32[32,1024]{1,0:T(8,128)S(1)}, f32[32,1024]{1,0:T(8,128)S(1)}, u32[]{:S(2)}, u32[]{:S(2)}) collective-permute-start(f32[32,1024]{1,0:T(8,128)S(1)} %fusion.6), channel_id=1, source_target_pairs={{32,0},{64,32},{96,64},{128,96},{160,128},{192,160},{224,192},{33,... | collective-permute-start | bytes 393224 | tf_op jit(solution)/shard_map/ppermute | solution.py:13
  219.7 0.6 copy-start.13
  220.4 138.2 %all-gather.18.cloned.1.call-start = ((), (), s32[]{:S(2)}) async-start(), calls=%async_computation.2 | async-start | bytes 4325376 | tf_op jit(solution)/shard_map/all_gather | solution.py:128
  220.9 156.4 %all-gather.24.cloned.1.call-start = ((), (), s32[]{:S(2)}) async-start(), calls=%async_computation.5 | async-start | bytes 1081344 | tf_op jit(solution)/shard_map/all_gather | solution.py:68
  226.0 60.7 %copy-start.26 = (u32[256]{0:T(256)S(1)}, u32[256]{0:T(256)}, u32[]{:S(2)}) copy-start(u32[256]{0:T(256)} %constant.218) | copy-start | bytes 3076
  226.5 129.6 %copy-start.5 = (f32[1024,256]{1,0:T(8,128)S(1)}, f32[1024,256]{1,0:T(8,128)}, u32[]{:S(2)}) copy-start(f32[1024,256]{1,0:T(8,128)} %all-gather.20.cloned.1.call-done) | copy-start | bytes 3145732
  229.1 208.2 %all-gather.30.cloned.1.call-start = ((), (), s32[]{:S(2)}) async-start(), calls=%async_computation.8 | async-start | bytes 8650752 | tf_op jit(solution)/shard_map/all_gather | solution.py:72
  231.1 291.4 %all-gather.26.cloned.1.call-start = ((), (), s32[]{:S(2)}) async-start(), calls=%async_computation.6 | async-start | bytes 4325376 | tf_op jit(solution)/shard_map/all_gather | solution.py:82
  287.9 98.9 %copy-start.24 = (f32[128]{0:T(128)}, f32[128]{0:T(128)S(1)}, u32[]{:S(2)}) copy-start(f32[128]{0:T(128)S(1)} %slice_bitcast_fusion.11) | copy-start | bytes 1540
  288.1 98.8 %copy-start.21 = (f32[1,128]{1,0:T(1,128)}, f32[1,128]{1,0:T(1,128)S(1)}, u32[]{:S(2)}) copy-start(f32[1,128]{1,0:T(1,128)S(1)} %fusion.72) | copy-start | bytes 1540
  288.1 68.6 %collective-permute-start.2 = (f32[256]{0:T(256)S(1)}, f32[256]{0:T(256)S(1)}, u32[]{:S(2)}, u32[]{:S(2)}) collective-permute-start(f32[256]{0:T(256)S(1)} %pad_maximum_fusion.5), channel_id=1, source_target_pairs={{32,0},{64,32},{96,64},{128,96},{160,128},{192,160},{224,192},{33,... | collective-permute-start | bytes 3080 | tf_op jit(solution)/shard_map/ppermute | solution.py:13
  292.1 228.7 %collective-permute-start.3 = (f32[32]{0:T(128)}, f32[32]{0:T(128)}, u32[]{:S(2)}, u32[]{:S(2)}) collective-permute-start(f32[32]{0:T(128)} %fusion.16), channel_id=1, source_target_pairs={{32,0},{64,32},{96,64},{128,96},{160,128},{192,160},{224,192},{33,... | collective-permute-start | bytes 392 | tf_op jit(solution)/shard_map/ppermute | solution.py:13
  356.1 8.0 %copy-start.18 = (f32[1024]{0:T(1024)}, f32[1024]{0:T(1024)S(1)}, u32[]{:S(2)}) copy-start(f32[1024]{0:T(1024)S(1)} %all-reduce.1) | copy-start | bytes 12292
  357.3 165.2 %collective-permute-start.4 = (f32[32,1024]{1,0:T(8,128)S(1)}, f32[32,1024]{1,0:T(8,128)}, u32[]{:S(2)}, u32[]{:S(2)}) collective-permute-start(f32[32,1024]{1,0:T(8,128)S(1)} %fusion.12), channel_id=1, source_target_pairs={{32,0},{64,32},{96,64},{128,96},{160,128},{192,160},{224,192},{33,... | collective-permute-start | bytes 393224 | tf_op jit(solution)/shard_map/ppermute | solution.py:13
  437.3 40.6 %copy-start.27 = (s32[2]{0:T(128)S(1)}, s32[2]{0:T(128)}, u32[]{:S(2)}) copy-start(s32[2]{0:T(128)} %iota_multiply_fusion) | copy-start | bytes 28
  503.8 0.7 copy-start.9
  506.5 7.2 %copy-start.15 = (f32[32,128]{1,0:T(8,128)S(1)}, f32[32,128]{1,0:T(8,128)}, u32[]{:S(2)}) copy-start(f32[32,128]{1,0:T(8,128)} %copy-done.14) | copy-start | bytes 49156
  506.5 7.8 %copy-start.16 = (f32[1,32,128]{2,1,0:T(8,128)S(1)}, f32[1,32,128]{2,1,0:T(8,128)}, u32[]{:S(2)}) copy-start(f32[1,32,128]{2,1,0:T(8,128)} %copy.41) | copy-start | bytes 49156
  506.5 7.8 %copy-start.17 = (f32[1,32,128]{2,1,0:T(8,128)S(1)}, f32[1,32,128]{2,1,0:T(8,128)}, u32[]{:S(2)}) copy-start(f32[1,32,128]{2,1,0:T(8,128)} %fusion.177) | copy-start | bytes 49156
  506.8 9.7 %copy-start.8 = (f32[32,1024]{1,0:T(8,128)S(1)}, f32[32,1024]{1,0:T(8,128)}, u32[]{:S(2)}) copy-start(f32[32,1024]{1,0:T(8,128)} %copy-done.7) | copy-start | bytes 393220
  506.8 9.7 %copy-start.4 = (f32[1024,1024]{1,0:T(8,128)S(1)}, f32[1024,1024]{1,0:T(8,128)}, u32[]{:S(2)}) copy-start(f32[1024,1024]{1,0:T(8,128)} %all-gather.18.cloned.1.call-done) | copy-start | bytes 12582916
  513.6 7.2 %copy-start.19 = (f32[1024]{0:T(1024)S(1)}, f32[1024]{0:T(1024)}, u32[]{:S(2)}) copy-start(f32[1024]{0:T(1024)} %copy-done.18) | copy-start | bytes 12292
Sparse Core Ops, SparseCore 0:
  10.6 54.3 all-gather.13
  68.1 48.2 all-gather.27
  119.5 50.5 all-gather.21
  173.1 47.3 all-gather.19
  222.8 50.4 all-gather.15
  276.4 50.5 all-gather.17
  330.1 47.2 all-gather.23
  379.9 57.2 all-gather.29
  439.8 51.3 all-gather.25
